TPU v7x, 32 devices: a whole 2x2x4 slice. The times are simulated.
32 devices in a mesh: groups: 2 (over x), example: 8 (over z, y), cls: 2 (over core).
Axes of the slice: x: 2, y: 2, z: 4, core: 2. Of those that a mesh axis runs over, the one named last changes fastest.
Arguments:
- features: bfloat16 [2048, 4096], P(('groups', 'example'), 'cls'), parts along dimension 0
- weights: float32 [8192, 8192], P(('groups', 'cls'), 'example'), parts along dimension 0
- labels: int32 [2048], P(('groups', 'example')), parts along dimension 0, may hold values from 0 to 8191
- counts: int32 [16], P(('groups', 'example')), parts along dimension 0, may hold values from 16 to 128, as said below
- active: int32 [2], P('groups'), parts along dimension 0, may hold values from 4096 to 8192
Outputs:
- moved: float32 [8192, 8192], P(('groups', 'cls'), 'example'), parts along dimension 0
- losses: float32 [2048], P(('groups', 'example')), parts along dimension 0
There are 2 independent parts, one for each index of `groups`. A program takes and returns all parts, laid end to end along the dimension named above; each array names one. Nothing has to cross between parts.
Inputs may be any that keep to these rules, and one draw needn't show every extreme that they name: `counts`: each block has at least 16 valid slots; some block is full in every draw.
All inputs are finite; a program needn't handle non-finite values.
Results may differ from a plain program's by a relative error of at most 0.006.
Values may be sent and summed in bfloat16 or wider, within the bound.
A program may use at most 128 MiB of HBM per device.

v0:
```python
import jax
import jax.numpy as jnp
from jax import lax
from jax.sharding import PartitionSpec as P

FEATURES = 4096
CLASSES = 8192
ITERS = 2


NEGATIVE = -1e30
LEARNING_RATE = 2e-05
DAMPING_SHARE = 0.1
EPSILON = 1e-06


def body(features, weights, labels, counts, active):
    gathered, labels_all, counts_all = (
        lax.all_gather(features, "example", axis=0, tiled=True),
        lax.all_gather(labels, "example", axis=0, tiled=True),
        lax.all_gather(counts, "example", axis=0, tiled=True),
    )
    all_rows = gathered.shape[0]
    per_device = features.shape[0]
    local_classes = weights.shape[1]
    row_index = jnp.arange(all_rows)
    owner = row_index // per_device
    blocks = jnp.arange(counts_all.shape[0])
    row_limit = jnp.sum(
        jnp.where(owner[:, None] == blocks[None, :], counts_all[None, :], 0), axis=1
    )
    is_valid = (row_index % per_device < row_limit).astype(jnp.float32)
    valid_total = jnp.sum(counts_all).astype(jnp.float32)
    active_count = active[0]
    class_index = lax.axis_index("example") * local_classes + jnp.arange(local_classes)
    is_active = class_index < active_count
    target = (labels_all % active_count).astype(jnp.int32)
    squares = gathered * gathered
    current = weights
    moved = jnp.zeros_like(weights)
    denominator = None
    losses_all = None
    for iteration in range(ITERS):
        current_low = current.astype(jnp.bfloat16)
        logits = lax.psum_scatter(
            jnp.dot(gathered, current_low, preferred_element_type=jnp.float32),
            "cls",
            scatter_dimension=0,
            tiled=True,
        )
        row_start = lax.axis_index("cls") * logits.shape[0]
        row_number = logits.shape[0]
        row_valid = lax.dynamic_slice_in_dim(is_valid, row_start, row_number, 0)
        row_target = lax.dynamic_slice_in_dim(target, row_start, row_number, 0)
        is_label = class_index[None, :] == row_target[:, None]
        masked = jnp.where(is_active[None, :], logits, NEGATIVE)
        local_peak = jnp.max(masked, axis=1)
        local_label = jnp.sum(jnp.where(is_label, logits, 0.0), axis=1)
        row_peak = lax.pmax(local_peak, "example")
        exponent = jnp.exp(masked - row_peak[:, None])
        row_total, label_logit = lax.psum((jnp.sum(exponent, axis=1), local_label), "example")
        probability = exponent / row_total[:, None]
        residual = (
            row_valid[:, None] * (probability - is_label.astype(jnp.float32)) / valid_total
        ).astype(jnp.bfloat16)
        losses_all = row_valid * (row_peak + jnp.log(row_total) - label_logit)
        fisher_weight = None
        if iteration == 0:
            fisher_weight = (
                row_valid[:, None] * probability * (1.0 - probability) / valid_total
            ).astype(jnp.bfloat16)
        if iteration == 0:
            residual, fisher_weight, losses_all = (
                lax.all_gather(residual, "cls", axis=0, tiled=True),
                lax.all_gather(fisher_weight, "cls", axis=0, tiled=True),
                lax.all_gather(losses_all.astype(jnp.bfloat16), "cls", axis=0, tiled=True).astype(
                    losses_all.dtype
                ),
            )
        else:
            residual, losses_all = (
                lax.all_gather(residual, "cls", axis=0, tiled=True),
                lax.all_gather(losses_all.astype(jnp.bfloat16), "cls", axis=0, tiled=True).astype(
                    losses_all.dtype
                ),
            )
        gradient = lax.dot_general(
            gathered, residual, (((0,), (0,)), ((), ())), preferred_element_type=jnp.float32
        )
        if iteration == 0:
            fisher = lax.dot_general(
                squares, fisher_weight, (((0,), (0,)), ((), ())), preferred_element_type=jnp.float32
            )
            fisher_sum = lax.psum(jnp.sum(fisher), ("example", "cls"))
            damping = DAMPING_SHARE * fisher_sum / (FEATURES * CLASSES) + EPSILON
            denominator = fisher + damping
        change = gradient / denominator
        current = current - LEARNING_RATE * change
        moved = moved - change
    own_losses = lax.dynamic_slice_in_dim(
        losses_all, lax.axis_index("example") * per_device, per_device, 0
    )
    return (moved, own_losses)


def solution(mesh):
    return jax.shard_map(
        body,
        mesh=mesh,
        in_specs=(
            P(("groups", "example"), "cls"),
            P(("groups", "cls"), "example"),
            P(("groups", "example")),
            P(("groups", "example")),
            P("groups"),
        ),
        out_specs=(P(("groups", "cls"), "example"), P(("groups", "example"))),
        check_vma=False,
    )
```

profile of v0, /device:TPU:0, one launch (start us, length us, event | category | flops | bytes accessed | tf_op | source)
XLA Modules:
  0.0 353.1 jit_solution(9420997783361034570)
XLA Ops:
  7.2 0.0 all-gather.7.cloned.1.call-start
  7.2 0.7 all-gather.7.cloned.1.call-update
  7.9 0.0 reduce-scatter.3.cloned.1.call-start
  7.9 77.7 %all-gather.7.cloned.1.call-done = bf16[1024,2048]{1,0:T(8,128)(2,1)} async-done(((bf16[128,2048]{1,0:T(8,128)(2,1)}), bf16[1024,2048]{1,0:T(8,128)(2,1)}) %all-gather.7.cloned.1.call-update) | async-done | bytes 4194320 | tf_op jit(solution)/shard_map/all_gather | solution.py:19
  85.6 11.2 %fusion.5 = f32[1024,1024]{1,0:T(8,128)} fusion(bf16[1024,2048]{1,0:T(8,128)(2,1)} %all-gather.7.cloned.1.call-done, f32[2048,1024]{1,0:T(8,128)} %param.6), kind=kOutput, calls=%fused_computation.8 | convolution fusion | flops 4297064448 | bytes 16777216 | tf_op jit(solution)/shard_map/dot_general | solution.py:46
  96.8 0.0 copy-start.4
  96.8 0.0 copy-start.2
  96.8 0.0 reduce-scatter.3.cloned.1.call-update
  96.8 0.0 all-gather.11.cloned.1.call-start
  97.5 0.0 copy-done.4
  97.5 0.6 dynamic-slice
  98.1 0.8 dynamic-update-slice
  98.9 9.9 %all-reduce = s32[8]{0:T(128)S(1)} all-reduce(s32[8]{0:T(128)S(1)} %dynamic-update-slice), channel_id=1, replica_groups=mesh['groups'=2,'example'=8,'cls'=2] {'example'}, use_global_device_ids=true, to_apply=%add | all-reduce | flops 8 | bytes 64
  109.4 0.6 reduce_sum.56
  110.7 0.0 copy-done.2
  110.7 18.2 %all-gather = s32[8,1,128]{2,1,0:T(1,128)S(1)} all-gather(s32[1,1,128]{2,1,0:T(1,128)S(1)} %bitcast.28), channel_id=1, replica_groups=mesh['groups'=2,'example'=8,'cls'=2] {'example'}, dimensions={0}, use_global_device_ids=true | all-gather | bytes 4608 | tf_op jit(solution)/shard_map/all_gather | solution.py:20
  128.9 0.1 broadcast_remainder_fusion
  129.1 0.1 dynamic_slice.12
  129.2 0.1 select_reduce_fusion.2
  129.3 0.1 dynamic_slice.11
  129.3 0.0 reduce-scatter.3.cloned.1.call-done
  129.4 0.0 copy-start
  129.4 2.0 select_reduce_fusion.1
  131.4 17.2 %pmax.14 = f32[512]{0:T(512)S(1)} all-reduce(f32[512]{0:T(512)S(1)} %select_reduce_fusion.1), channel_id=1, replica_groups=mesh['groups'=2,'example'=8,'cls'=2] {'example'}, use_global_device_ids=true, to_apply=%region_3.4 | all-reduce | flops 512 | bytes 4096 | tf_op jit(solution)/shard_map/pmax | solution.py:59
  148.6 0.0 copy-done
  148.6 0.5 fusion.16
  149.1 19.1 %psum.28 = f32[512]{0:T(512)S(1)} all-reduce(f32[512]{0:T(512)S(1)} %fusion.16), channel_id=1, replica_groups=mesh['groups'=2,'example'=8,'cls'=2] {'example'}, use_global_device_ids=true, to_apply=%region_5.6 | all-reduce | flops 512 | bytes 4096 | tf_op jit(solution)/shard_map/psum | solution.py:61
  168.1 2.8 fusion.13
  170.9 0.0 all-gather.11.cloned.1.call-update
  170.9 0.0 all-gather.9.cloned.1.call-start
  171.0 0.5 all-gather.9.cloned.1.call-update
  171.5 0.0 reduce-scatter.5.cloned.1.call-start
  171.6 9.2 %copy.16 = f32[2048,1024]{0,1:T(8,128)} copy(f32[2048,1024]{1,0:T(8,128)} %param.6) | data formatting | bytes 16777216 | tf_op args[1]
  180.8 0.0 all-gather.11.cloned.1.call-done
  180.8 11.4 %fusion.26 = (f32[]{:T(128)}, f32[2048,1024]{1,0:T(8,128)}) fusion(bf16[1024,1024]{1,0:T(8,128)(2,1)} %all-gather.11.cloned.1.call-done, bf16[1024,2048]{1,0:T(8,128)(2,1)} %all-gather.7.cloned.1.call-done), kind=kOutput, calls=%fused_computation.49 | convolution fusion | flops 4299161600 | bytes 14680068 | tf_op jit(solution)/shard_map/dot_general | solution.py:91
  192.2 33.1 %psum.29 = f32[]{:T(128)} all-reduce(f32[]{:T(128)} %get-tuple-element.14), channel_id=1, replica_groups=mesh['groups'=2,'example'=8,'cls'=2] {'example','cls'}, use_global_device_ids=true, to_apply=%region_8.9 | all-reduce | flops 1 | bytes 8 | tf_op jit(solution)/shard_map/psum | solution.py:94
  225.4 9.1 %copy.15 = f32[2048,1024]{0,1:T(8,128)} copy(f32[2048,1024]{1,0:T(8,128)} %get-tuple-element.15) | data formatting | bytes 16777216 | tf_op jit(solution)/shard_map/dot_general | solution.py:91
  235.1 0.0 all-gather.9.cloned.1.call-done
  235.2 0.0 copy-start.3
  235.2 10.1 %bitcast_divide_fusion.1 = f32[2048,1024]{0,1:T(8,128)S(1)} fusion(f32[2048,1024]{0,1:T(8,128)} %copy.15, bf16[1024,1024]{1,0:T(8,128)(2,1)} %all-gather.9.cloned.1.call-done, bf16[1024,2048]{1,0:T(8,128)(2,1)} %all-gather.7.cloned.1.call-done, f32[]{:T(128)S(6)} %add.68), kind=kOutput, calls=%fused_computation.2 | convolution fusion | flops 4299161600 | bytes 23068676 | tf_op jit(solution)/shard_map/dot_general | solution.py:87
  245.3 0.0 copy-start.5
  245.3 3.4 copy-done.5
  248.7 0.0 copy-done.3
  248.7 9.5 %fusion.7 = f32[1024,1024]{1,0:T(8,128)} fusion(bf16[1024,2048]{1,0:T(8,128)(2,1)S(1)} %copy-done.3, f32[2048,1024]{0,1:T(8,128)} %copy.16, f32[2048,1024]{0,1:T(8,128)S(1)} %bitcast_divide_fusion.1), kind=kOutput, calls=%fused_computation.13 | convolution fusion | flops 4301258752 | bytes 25165824 | tf_op jit(solution)/shard_map/dot_general | solution.py:46
  258.2 0.0 reduce-scatter.5.cloned.1.call-update
  258.3 0.0 all-gather.13.cloned.1.call-start
  258.3 9.4 %reduce-scatter.5.cloned.1.call-done = f32[512,1024]{1,0:T(8,128)} async-done(((f32[1024,1024]{1,0:T(8,128)}), f32[512,1024]{1,0:T(8,128)}) %reduce-scatter.5.cloned.1.call-update) | async-done | bytes 2097168 | tf_op jit(solution)/shard_map/reduce_scatter | solution.py:45
  267.7 0.0 copy-start.1
  267.7 2.0 select_reduce_fusion
  269.7 21.7 %pmax.15 = f32[512]{0:T(512)S(1)} all-reduce(f32[512]{0:T(512)S(1)} %select_reduce_fusion), channel_id=1, replica_groups=mesh['groups'=2,'example'=8,'cls'=2] {'example'}, use_global_device_ids=true, to_apply=%region_11.12 | all-reduce | flops 512 | bytes 4096 | tf_op jit(solution)/shard_map/pmax | solution.py:59
  291.4 0.0 copy-done.1
  291.4 0.7 fusion.8
  292.2 17.2 %all-reduce.1 = (f32[512]{0:T(512)S(1)}, f32[512]{0:T(512)S(1)}) all-reduce(f32[512]{0:T(512)S(1)} %get-tuple-element.9, f32[512]{0:T(512)S(1)} %get-tuple-element.8), channel_id=1, replica_groups=mesh['groups'=2,'example'=8,'cls'=2] {'example'}, use_global_device_ids=true, to_apply=%region_13.14 | all-reduce | flops 1024 | bytes 8192 | tf_op jit(solution)/shard_map/psum | solution.py:61
  309.3 2.1 fusion.14
  311.5 0.0 all-gather.13.cloned.1.call-update
  311.5 0.1 multiply_convert_fusion
  311.6 2.0 all-gather.1
  313.6 0.6 dynamic_slice.13
  314.2 6.6 %all-gather.13.cloned.1.call-done = bf16[1024,1024]{1,0:T(8,128)(2,1)} async-done(((bf16[512,1024]{1,0:T(8,128)(2,1)}), bf16[1024,1024]{1,0:T(8,128)(2,1)}) %all-gather.13.cloned.1.call-update) | async-done | bytes 2097168 | tf_op jit(solution)/shard_map/all_gather | solution.py:82
  320.9 16.2 %fusion = f32[2048,1024]{0,1:T(8,128)} fusion(f32[2048,1024]{0,1:T(8,128)} %copy-done.5, f32[2048,1024]{0,1:T(8,128)} %copy.15, bf16[1024,1024]{1,0:T(8,128)(2,1)} %all-gather.13.cloned.1.call-done, bf16[1024,2048]{1,0:T(8,128)(2,1)} %all-gather.7.cloned.1.call-done, f32[]{:T(128)S(6)} %add.68), kind=kOutput, calls=%fused_computation.1 | convolution fusion | flops 4303355904 | bytes 31457284 | tf_op jit(solution)/shard_map/dot_general | solution.py:87
  337.1 9.2 %copy.18 = f32[2048,1024]{1,0:T(8,128)} copy(f32[2048,1024]{0,1:T(8,128)} %fusion) | data formatting | bytes 16777216
  (8 shorter events, 0.0 us)
Async XLA Ops:
  7.2 78.5 %all-gather.7.cloned.1.call-start = ((), (), s32[]{:S(2)}) async-start(), calls=%async_computation.2 | async-start | bytes 4718592 | tf_op jit(solution)/shard_map/all_gather | solution.py:19
  7.9 121.5 %reduce-scatter.3.cloned.1.call-start = ((), (), s32[]{:S(2)}) async-start(), calls=%async_computation.3 | async-start | bytes 6291456 | tf_op jit(solution)/shard_map/reduce_scatter | solution.py:45
  96.8 0.7 copy-start.4
  96.8 13.9 %copy-start.2 = (s32[128]{0:T(128)S(1)}, s32[128]{0:T(128)}, u32[]{:S(2)}) copy-start(s32[128]{0:T(128)} %param.7) | copy-start | bytes 1540
  96.8 84.0 %all-gather.11.cloned.1.call-start = ((), (), s32[]{:S(2)}) async-start(), calls=%async_computation.5 | async-start | bytes 3145728 | tf_op jit(solution)/shard_map/all_gather | solution.py:75
  129.4 19.2 %copy-start = (f32[512,1024]{1,0:T(8,128)S(1)}, f32[512,1024]{1,0:T(8,128)}, u32[]{:S(2)}) copy-start(f32[512,1024]{1,0:T(8,128)} %reduce-scatter.3.cloned.1.call-done) | copy-start | bytes 6291460
  170.9 64.2 %all-gather.9.cloned.1.call-start = ((), (), s32[]{:S(2)}) async-start(), calls=%async_computation.4 | async-start | bytes 3145728 | tf_op jit(solution)/shard_map/all_gather | solution.py:74
  171.5 96.2 %reduce-scatter.5.cloned.1.call-start = ((), (), s32[]{:S(2)}) async-start(), calls=%async_computation.6 | async-start | bytes 6291456 | tf_op jit(solution)/shard_map/reduce_scatter | solution.py:45
  235.2 13.5 %copy-start.3 = (bf16[1024,2048]{1,0:T(8,128)(2,1)S(1)}, bf16[1024,2048]{1,0:T(8,128)(2,1)}, u32[]{:S(2)}) copy-start(bf16[1024,2048]{1,0:T(8,128)(2,1)} %all-gather.7.cloned.1.call-done) | copy-start | bytes 12582916
  245.3 3.4 copy-start.5
  258.3 62.6 %all-gather.13.cloned.1.call-start = ((), (), s32[]{:S(2)}) async-start(), calls=%async_computation.7 | async-start | bytes 3145728 | tf_op jit(solution)/shard_map/all_gather | solution.py:82
  267.7 23.7 %copy-start.1 = (f32[512,1024]{1,0:T(8,128)S(1)}, f32[512,1024]{1,0:T(8,128)}, u32[]{:S(2)}) copy-start(f32[512,1024]{1,0:T(8,128)} %reduce-scatter.5.cloned.1.call-done) | copy-start | bytes 6291460
Sparse Core Ops, SparseCore 0:
  10.1 75.5 all-gather.6
  97.0 10.5 reduce-scatter.2
  171.1 7.7 all-gather.10
  180.3 11.7 all-gather.8
  258.4 9.2 reduce-scatter.4
  311.6 9.2 all-gather.12
where the time goes:
time: 354 us; the launch traced here: 353 us
  blocking collectives  138 us (39%)
  waiting for transfers between devices  95 us (27%)
  matrix products  58.4 us (16%)
  local copies, waits for them, and re-layouts  33.1 us (9%)
  between operations  16.8 us (5%)
  other arithmetic  11.1 us (3%)
    all_gather x1, waiting for transfers between devices, body(): lax.all_gather(features, 'example', axis=0, tiled=True)  77.7 us
    pmax x2, blocking collectives, body(): row_peak = lax.pmax(local_peak, 'example')  38.9 us
    psum x2, blocking collectives, body(): lax.psum((jnp.sum(exponent, axis=1), local_label), 'example')  36.3 us
    psum x1, blocking collectives, body(): fisher_sum = lax.psum(jnp.sum(fisher), ('example', 'cls'))  33.1 us
    dot_general x2, matrix products, body(): lax.dot_general(gathered, residual, (((0,), (0,)), ((), ())), preferred_e...  26.3 us
    unnamed x18, local copies, waits for them, and re-layouts  23.2 us
    dot_general x2, matrix products, body(): jnp.dot(gathered, current_low, preferred_element_type=jnp.float32)  20.7 us
    all_gather x1, blocking collectives, body(): lax.all_gather(labels, 'example', axis=0, tiled=True)  18.2 us
  transfers between devices with their start and end apart: 6, of which 3 were waited for; matrix products, arithmetic and copies ran while one was open for 9% of the time, Pallas kernels for 0%

commit v1 on v0

v1 whole, which is shorter than its diff:
```python
import functools

import jax
import jax.numpy as jnp
from jax import lax
from jax.experimental import pallas as pl
from jax.experimental.pallas import tpu as pltpu
from jax.sharding import PartitionSpec as P

ITERS = 2
NEGATIVE = -1e30
LEARNING_RATE = 2e-05
DAMPING_SHARE = 0.1
EPSILON = 1e-06
MESH = pl.DeviceIdType.MESH
UP, DOWN, SIDE, SIBLING = 0, 1, 2, 3
F32, BF16 = jnp.float32, jnp.bfloat16


def kernel(
    Z, Y, scale,
    features, weights, meta, active,
    moved, losses,
    x, xt, w, wlow, e_scr, r_scr, fw_scr, rec, g_scr,
    meta_all, stat1, stat2, damp_all, b_scr, ssq, loss_scr,
    own_sem, w_sem, gsend, grecv, wsend, wrecv, msend, mrecv,
    ssend, srecv, dsend, drecv, out_sem, osend, orecv,
):
    n = Z * Y
    nd = 2 * n
    rows_n = features.shape[0]
    half = features.shape[1]
    all_rows = n * rows_n
    ck = w.shape[2]
    me = lax.axis_index("example")
    k = lax.axis_index("cls")
    sib = 1 - k
    z, y = me // Y, lax.rem(me, Y)
    mine = me * 2 + k

    def rows(slot):
        return pl.ds(pl.multiple_of(slot * rows_n, rows_n), rows_n)

    def columns(index):
        return pl.ds(pl.multiple_of(index * ck, ck), ck)

    def remote(src, dst, ssem, rsem, example, core):
        return pltpu.make_async_remote_copy(
            src_ref=src, dst_ref=dst, send_sem=ssem, recv_sem=rsem,
            device_id={"example": example, "cls": core}, device_id_type=MESH,
        )

    own_copy = pltpu.make_async_copy(features, x.at[k, rows(me)], own_sem)
    own_copy.start()
    w_copy = pltpu.make_async_copy(weights.at[:, columns(k)], w.at[k], w_sem)
    w_copy.start()

    barrier = pltpu.get_barrier_semaphore()

    def greet(p, c):
        peer = lax.rem(mine + p, nd)
        pl.semaphore_signal(
            barrier, inc=1, device_id={"example": peer // 2, "cls": lax.rem(peer, 2)},
            device_id_type=MESH,
        )
        return c

    lax.fori_loop(1, nd, greet, 0)
    pl.semaphore_wait(barrier, nd - 1)

    def forward(slot, direction, src):
        target, core = {
            UP: (me + Y, k),
            DOWN: (me - Y, k),
            SIDE: (z * Y + (Y - 1 - y), k),
            SIBLING: (me, sib),
        }[direction]
        return remote(
            src, x.at[k, rows(slot)], gsend.at[direction, slot], grecv.at[k, slot], target, core
        )

    def landed(h, slot):
        remote(
            x.at[h, rows(slot)], x.at[h, rows(slot)], gsend.at[SIBLING, slot],
            grecv.at[h, slot], me, sib,
        ).wait_recv()

    meta_all[me] = meta[...]

    def meta_copy(p):
        peer = lax.rem(me + p, n)
        return peer, remote(
            meta, meta_all.at[me], msend.at[p], mrecv.at[me], peer, k
        )

    def meta_start(p, c):
        meta_copy(p)[1].start()
        return c

    def line(j, act, own=False):
        for sign in (1,) if own else (-1, 1):
            zz = z + sign * j
            slot = zz * Y + y
            src = features if own else x.at[k, rows(slot)]
            inside = jnp.logical_and(zz >= 0, zz < Z)

            @pl.when(inside)
            def _():
                act("enter", slot, None)
                if own or sign == -1:
                    @pl.when(z < Z - 1)
                    def _():
                        act("send", slot, forward(slot, UP, src))
                if own or sign == 1:
                    @pl.when(z > 0)
                    def _():
                        act("send", slot, forward(slot, DOWN, src))
                if Y == 2:
                    act("send", slot, forward(slot, SIDE, src))
                act("send", slot, forward(slot, SIBLING, src))

    def begin(kind, slot, copy):
        if kind == "enter":
            landed(k, slot)
        else:
            copy.start()

    def begin_own(kind, slot, copy):
        if kind == "send":
            copy.start()

    def finish(kind, slot, copy):
        if kind == "send":
            copy.wait_send()

    line(0, begin_own, own=True)
    lax.fori_loop(1, n, meta_start, 0)
    w_send = remote(weights.at[:, columns(sib)], w.at[k], wsend, wrecv, me, sib)
    w_send.start()

    def lower(h):
        step = min(512, half)

        def go(i, c):
            part = pl.ds(pl.multiple_of(i * step, step), step)
            wlow[h, part, :] = w[h, part, :].astype(BF16)
            return c

        lax.fori_loop(0, half // step, go, 0)

    w_copy.wait()
    lower(k)
    own_copy.wait()
    remote(w.at[sib], w.at[sib], wsend, wrecv, me, sib).wait_recv()
    lower(sib)

    def meta_wait(p, c):
        src = lax.rem(me + p, n)
        remote(meta, meta_all.at[src], msend.at[p], mrecv.at[src], me, sib).wait_recv()
        return c

    lax.fori_loop(1, n, meta_wait, 0)

    active_count = active[0]
    class_base = mine * ck
    class_index = class_base + lax.broadcasted_iota(jnp.int32, (rows_n, ck), 1)
    class_float = class_index.astype(F32)
    is_active = class_index < active_count
    lane = lax.broadcasted_iota(jnp.int32, (rows_n, rows_n), 1)

    def column(row):
        return jnp.broadcast_to(row, (rows_n, rows_n)).T[:, 0:1]

    def statistics(slot, logits, stat, with_label):
        masked = jnp.where(is_active, logits, NEGATIVE)
        peak = jnp.max(masked, axis=1, keepdims=True)
        exponent = jnp.exp(masked - peak)
        total = jnp.sum(exponent, axis=1, keepdims=True)
        e_scr[rows(slot), :] = exponent
        tile = jnp.where(lane == 0, peak, total)
        if with_label:
            target = column(meta_all[slot, 0:1, :])
            label = jnp.sum(
                jnp.where(class_float == target, logits, 0.0), axis=1, keepdims=True
            )
            tile = jnp.where(lane == 2, label, tile)
        tile = tile.T
        stat[mine, 0, pl.ds(slot, 1), :] = tile[0:1, :]
        stat[mine, 1, pl.ds(slot, 1), :] = tile[1:2, :]
        if with_label:
            stat[mine, 2, pl.ds(slot, 1), :] = tile[2:3, :]

    def process(slot):
        logits = None
        squares = None
        for h in range(2):
            block = x[h, rows(slot), :]
            xt[h, :, rows(slot)] = block.T
            term = jnp.sum((block * block).astype(F32), axis=1, keepdims=True)
            part = jnp.dot(block, wlow[h], preferred_element_type=F32)
            squares = term if h == 0 else squares + term
            logits = part if h == 0 else logits + part
        ssq[rows(slot), :] = jnp.broadcast_to(squares, (rows_n, 128))
        statistics(slot, logits, stat1, False)

    quarters = 2 * Y

    def gather(t, c):
        j, q = t // quarters, lax.rem(t, quarters)

        @pl.when(q == quarters - 2)
        def _():
            line(j + 1, begin)

        zz = z + (2 * lax.rem(q, 2) - 1) * j
        yy = y if Y == 1 else jnp.where(q < 2, y, 1 - y)
        slot = zz * Y + yy
        inside = jnp.logical_and(zz >= 0, zz < Z)
        inside = jnp.logical_and(inside, jnp.logical_or(j > 0, lax.rem(q, 2) == 1))

        @pl.when(inside)
        def _():
            if Y == 2:
                @pl.when(q >= 2)
                def _():
                    landed(k, slot)
                    forward(slot, SIBLING, x.at[k, rows(slot)]).start()

            landed(sib, slot)
            process(slot)

        return c

    lax.fori_loop(0, Z * quarters, gather, 0)

    def share(buffer, count, ssem, rsem):
        def piece(slot):
            return buffer.at[slot] if count is None else buffer.at[slot, pl.ds(0, count)]

        def copy(p):
            peer = lax.rem(mine + p, nd)
            return remote(
                piece(mine), piece(mine), ssem.at[p], rsem.at[mine], peer // 2, lax.rem(peer, 2)
            )

        def start(p, c):
            copy(p).start()
            return c

        def wait_in(p, c):
            src = lax.rem(mine + p, nd)
            remote(
                piece(src), piece(src), ssem.at[p], rsem.at[src], me, sib
            ).wait_recv()
            return c

        def wait_out(p, c):
            copy(p).wait_send()
            return c

        return (
            lambda: lax.fori_loop(1, nd, start, 0),
            lambda: lax.fori_loop(1, nd, wait_in, 0),
            lambda: lax.fori_loop(1, nd, wait_out, 0),
        )

    counts = meta_all[:, 1, :]
    valid_total = jnp.sum(counts[:, 0:1], axis=0, keepdims=True)

    def combine(stat):
        peak = stat[0, 0]
        for d in range(1, nd):
            peak = jnp.maximum(peak, stat[d, 0])
        total = jnp.zeros_like(peak)
        for d in range(nd):
            total = total + stat[d, 1] * jnp.exp(stat[d, 0] - peak)
        b_scr[...] = jnp.exp(stat[mine, 0] - peak) / total
        return peak, total

    row_number = lax.broadcasted_iota(jnp.int32, (rows_n, 1), 0).astype(F32)

    def residuals(first):
        def go(i, acc):
            valid = (row_number < meta_all[i, 1:2, 0:1]).astype(F32) / valid_total
            target = column(meta_all[i, 0:1, :])
            probability = e_scr[rows(i), :] * column(b_scr[pl.ds(i, 1), :])
            is_label = (class_float == target).astype(F32)
            r_scr[rows(i), :] = (valid * (probability - is_label)).astype(BF16)
            if first:
                fw = (valid * probability * (1.0 - probability)).astype(BF16)
                fw_scr[rows(i), :] = fw
                row_sum = jnp.sum(fw.astype(F32), axis=1, keepdims=True)
                acc = acc + jnp.sum(row_sum * ssq[rows(i), 0:1], axis=0, keepdims=True)
            return acc

        return lax.fori_loop(0, n, go, jnp.zeros((1, 1), F32))

    start1, in1, out1 = share(stat1, None, ssend.at[0], srecv.at[0])
    start1()
    in1()
    combine(stat1)
    fisher_part = residuals(True)
    damp_all[mine] = jnp.broadcast_to(fisher_part, damp_all.shape[1:])
    start_d, in_d, out_d = share(damp_all, None, dsend, drecv)
    start_d()

    step = min(512, half)
    per_half = half // step

    def chunk(i):
        return i // per_half, pl.ds(pl.multiple_of(lax.rem(i, per_half) * step, step), step)

    def gradient(i, c):
        h, part = chunk(i)
        g_scr[h, part, :] = jnp.dot(xt[h, part, :], r_scr[...], preferred_element_type=F32)
        return c

    lax.fori_loop(0, 2 * per_half, gradient, 0)

    in_d()
    fisher_sum = damp_all[0, 0:1, 0:1]
    for d in range(1, nd):
        fisher_sum = fisher_sum + damp_all[d, 0:1, 0:1]
    damping = DAMPING_SHARE * fisher_sum / scale + EPSILON
    e_scr[...] = jnp.zeros_like(e_scr)

    def fisher_step(i, c):
        h, part = chunk(i)
        block = xt[h, part, :]
        fisher = jnp.dot(block * block, fw_scr[...], preferred_element_type=F32)
        inverse = 1.0 / (fisher + damping)
        rec[h, part, :] = inverse
        change = g_scr[h, part, :] * inverse
        g_scr[h, part, :] = change
        low = (w[h, part, :] - LEARNING_RATE * change).astype(BF16)
        wlow[h, part, :] = low
        e_scr[...] += jnp.dot(x[h, :, part], low, preferred_element_type=F32)
        return c

    lax.fori_loop(0, 2 * per_half, fisher_step, 0)

    def second(i, c):
        statistics(i, e_scr[rows(i), :], stat2, True)
        return c

    lax.fori_loop(0, n, second, 0)
    start2, in2, out2 = share(stat2, None, ssend.at[1], srecv.at[1])
    start2()
    in2()
    peak, total = combine(stat2)
    label = stat2[0, 2]
    for d in range(1, nd):
        label = label + stat2[d, 2]
    lane_row = lax.broadcasted_iota(jnp.int32, (n, rows_n), 1).astype(F32)
    loss_scr[...] = (lane_row < counts).astype(F32) * (peak + jnp.log(total) - label)
    losses[...] = loss_scr[pl.ds(me, 1), :]
    residuals(False)

    def place(i):
        h = jnp.where(i < per_half, sib, k)
        return h, pl.ds(pl.multiple_of(lax.rem(i, per_half) * step, step), step)

    def out_remote(i):
        h, part = place(i)
        return remote(
            w.at[h, part, :], moved.at[part, columns(k)], osend.at[i], orecv.at[i], me, sib
        )

    def out_local(i):
        h, part = place(i)
        return pltpu.make_async_copy(
            w.at[h, part, :], moved.at[part, columns(k)], out_sem.at[i - per_half]
        )

    def last(i, c):
        h, part = place(i)
        grad = jnp.dot(xt[h, part, :], r_scr[...], preferred_element_type=F32)
        w[h, part, :] = -g_scr[h, part, :] - grad * rec[h, part, :]

        @pl.when(i < per_half)
        def _():
            out_remote(i).start()

        @pl.when(i >= per_half)
        def _():
            out_local(i).start()

        return c

    w_send.wait_send()
    lax.fori_loop(0, 2 * per_half, last, 0)

    line(0, finish, own=True)

    def drain(j, c):
        line(j, finish)
        return c

    lax.fori_loop(1, Z, drain, 0)
    if Y == 2:
        def drain_side(zz, c):
            slot = zz * Y + (1 - y)
            forward(slot, SIBLING, x.at[k, rows(slot)]).wait_send()
            return c

        lax.fori_loop(0, Z, drain_side, 0)

    def meta_done(p, c):
        meta_copy(p)[1].wait_send()
        return c

    lax.fori_loop(1, n, meta_done, 0)
    out1()
    out_d()
    out2()

    def out_done(i, c):
        out_remote(i).wait_send()
        _, part = place(i)
        remote(
            w.at[k, part, :], moved.at[part, columns(sib)], osend.at[i], orecv.at[i], me, sib
        ).wait_recv()
        out_local(i + per_half).wait()
        return c

    lax.fori_loop(0, per_half, out_done, 0)


def solution(mesh):
    n = mesh.shape["example"]
    Y = 2 if n == 8 else 1
    Z = n // Y
    nd = 2 * n

    def body(features, weights, labels, counts, active):
        rows_n, half = features.shape
        local = weights.shape[1]
        ck = local // 2
        all_rows = rows_n * n
        target = (labels % active[0]).astype(F32)
        meta = jnp.concatenate(
            [
                target[None, :],
                jnp.broadcast_to(counts.astype(F32)[:, None], (7, rows_n)),
            ],
            axis=0,
        )
        scale = float(half * 2 * local * n)
        per_half = half // min(512, half)
        dma = pltpu.SemaphoreType.DMA
        moved, losses = pl.pallas_call(
            functools.partial(kernel, Z, Y, scale),
            out_shape=(
                jax.ShapeDtypeStruct(weights.shape, F32),
                jax.ShapeDtypeStruct((1, rows_n), F32),
            ),
            in_specs=[
                pl.BlockSpec(memory_space=pl.ANY),
                pl.BlockSpec(memory_space=pl.ANY),
                pl.BlockSpec(memory_space=pltpu.VMEM),
                pl.BlockSpec(memory_space=pltpu.SMEM),
            ],
            out_specs=(
                pl.BlockSpec(memory_space=pl.ANY),
                pl.BlockSpec(memory_space=pltpu.VMEM),
            ),
            scratch_shapes=[
                pltpu.VMEM((2, all_rows, half), BF16),
                pltpu.VMEM((2, half, all_rows), BF16),
                pltpu.VMEM((2, half, ck), F32),
                pltpu.VMEM((2, half, ck), BF16),
                pltpu.VMEM((all_rows, ck), F32),
                pltpu.VMEM((all_rows, ck), BF16),
                pltpu.VMEM((all_rows, ck), BF16),
                pltpu.VMEM((2, half, ck), F32),
                pltpu.VMEM((2, half, ck), F32),
                pltpu.VMEM((n, 8, rows_n), F32),
                pltpu.VMEM((nd, 2, n, rows_n), F32),
                pltpu.VMEM((nd, 3, n, rows_n), F32),
                pltpu.VMEM((nd, 8, 128), F32),
                pltpu.VMEM((n, rows_n), F32),
                pltpu.VMEM((all_rows, 128), F32),
                pltpu.VMEM((n, rows_n), F32),
                dma, dma,
                dma((4, n)), dma((2, n)),
                dma, dma,
                dma((n,)), dma((n,)),
                dma((2, nd)), dma((2, nd)),
                dma((nd,)), dma((nd,)),
                dma((per_half,)), dma((per_half,)), dma((per_half,)),
            ],
            compiler_params=pltpu.CompilerParams(
                collective_id=0, has_side_effects=True, vmem_limit_bytes=67043328
            ),
        )(features, weights, meta, active)
        return moved, losses.reshape(rows_n)

    return jax.shard_map(
        body,
        mesh=mesh,
        in_specs=(
            P(("groups", "example"), "cls"),
            P(("groups", "cls"), "example"),
            P(("groups", "example")),
            P(("groups", "example")),
            P("groups"),
        ),
        out_specs=(P(("groups", "cls"), "example"), P(("groups", "example"))),
        check_vma=False,
    )
```

time: 354 us -> 117 us (0.33)
  blocking collectives: 138 us -> 0 us
  Pallas kernels: 0 us -> 105 us
  waiting for transfers between devices: 95 us -> 0 us
  matrix products: 58.4 us -> 0 us
  local copies, waits for them, and re-layouts: 33.1 us -> 9.56 us
  between operations: 16.8 us -> 1.95 us
  other arithmetic: 11.1 us -> 0.78 us
    pallas_call x0 -> x1, Pallas kernels: none -> 105 us  [body(): pl.pallas_call(functools.partial(kernel, Z, Y, scale), out_shape=(jax.Sha...]
    all_gather x4 -> x0, waiting for transfers between devices: 84.4 us -> none  [the longest x1 77.7 us: body(): lax.all_gather(features, 'example', axis=0, tiled=True)]
    psum x3 -> x0, blocking collectives: 69.4 us -> none  [the longest x2 36.3 us: body(): lax.psum((jnp.sum(exponent, axis=1), local_label), 'example')]
    dot_general x5 -> x0, matrix products: 58.4 us -> none  [the longest x2 26.3 us: body(): lax.dot_general(gathered, residual, (((0,), (0,)), ((), ())), preferred_e...]
    pmax x2 -> x0, blocking collectives: 38.9 us -> none  [body(): row_peak = lax.pmax(local_peak, 'example')]
    all_gather x2 -> x0, blocking collectives: 20.3 us -> none  [the longest x1 18.2 us: body(): lax.all_gather(labels, 'example', axis=0, tiled=True)]
    unnamed x18 -> x4, local copies, waits for them, and re-layouts: 23.2 us -> 8.96 us
    unnamed x1 -> x0, blocking collectives: 9.87 us -> none
  transfers between devices with their start and end apart: 6 -> 0, of which waited for: 3 -> 0; matrix products, arithmetic and copies ran while one was open for 9% -> 0% of each run, Pallas kernels for 0% -> 0%
where the time goes in v1:
time: 117 us
  Pallas kernels  105 us (90%)
  local copies, waits for them, and re-layouts  9.56 us (8%)
  between operations  1.95 us (2%)
    pallas_call x1, Pallas kernels, body(): pl.pallas_call(functools.partial(kernel, Z, Y, scale), out_shape=(jax.Sha...  105 us
    unnamed x4, local copies, waits for them, and re-layouts  8.96 us

profile of v1, /device:TPU:0, one launch (start us, length us, event | category | flops | bytes accessed | tf_op | source)
XLA Modules:
  0.0 116.8 jit_solution(6888881875611095009)
XLA Ops:
  1.9 0.8 convert_bitcast_fusion
  2.7 0.6 concatenate.3.meta
  3.3 104.5 %shard_map.68 = (f32[2048,1024]{1,0:T(8,128)}, f32[1,128]{1,0:T(1,128)}) custom-call(bf16[128,2048]{1,0:T(8,128)(2,1)} %features.1, f32[2048,1024]{1,0:T(8,128)} %weights.1, f32[8,128]{1,0:T(8,128)} %concatenate.3.meta, s32[1]{0:T(128)} %copy.10.active), custom_call_target="tpu_custom_call" | custom-call | tf_op jit(solution)/shard_map/pallas_call | solution.py:451
  107.9 0.0 copy-start
  107.9 8.4 %copy.11 = f32[2048,1024]{1,0:T(8,128)} copy(f32[2048,1024]{1,0:T(8,128)} %get-tuple-element.8) | data formatting | bytes 16777216
  116.3 0.0 copy-done
  116.3 0.5 copy.12
Async XLA Ops:
  107.9 8.5 %copy-start = (f32[1,128]{1,0:T(1,128)S(1)}, f32[1,128]{1,0:T(1,128)}, u32[]{:S(2)}) copy-start(f32[1,128]{1,0:T(1,128)} %get-tuple-element.5) | copy-start | bytes 1540

commit v2 on v1

--- a/solution.py
+++ b/solution.py
@@ -36,6 +36,7 @@
     k = lax.axis_index("cls")
     sib = 1 - k
     z, y = me // Y, lax.rem(me, Y)
+    is_end = jnp.logical_or(z == 0, z == Z - 1)
     mine = me * 2 + k
 
     def rows(slot):
@@ -68,7 +69,12 @@
     lax.fori_loop(1, nd, greet, 0)
     pl.semaphore_wait(barrier, nd - 1)
 
-    def forward(slot, direction, src):
+    def forward(slot, direction, src, second=None):
+        place = rows(slot)
+        if second is not None:
+            size = rows_n // 2
+            place = pl.ds(pl.multiple_of(slot * rows_n + second * size, size), size)
+            src = x.at[k, place]
         target, core = {
             UP: (me + Y, k),
             DOWN: (me - Y, k),
@@ -76,7 +82,7 @@
             SIBLING: (me, sib),
         }[direction]
         return remote(
-            src, x.at[k, rows(slot)], gsend.at[direction, slot], grecv.at[k, slot], target, core
+            src, x.at[k, place], gsend.at[direction, slot], grecv.at[k, slot], target, core
         )
 
     def landed(h, slot):
@@ -115,9 +121,43 @@
                     @pl.when(z > 0)
                     def _():
                         act("send", slot, forward(slot, DOWN, src))
-                if Y == 2:
+                if Y == 2 and own:
                     act("send", slot, forward(slot, SIDE, src))
+                elif Y == 2:
+                    far = jnp.logical_and(is_end, j == Z - 1)
+                    edge = jnp.logical_or(zz == 0, zz == Z - 1)
+                    near = jnp.logical_and(jnp.logical_not(is_end), edge)
+                    near = jnp.logical_and(near, j == 1)
+
+                    @pl.when(far)
+                    def _():
+                        act("send", slot, forward(slot, SIDE, src, 0))
+
+                    @pl.when(jnp.logical_not(jnp.logical_or(far, near)))
+                    def _():
+                        act("send", slot, forward(slot, SIDE, src))
                 act("send", slot, forward(slot, SIBLING, src))
+
+    def cross(j, slot, act):
+        src = x.at[k, rows(slot)]
+
+        @pl.when(jnp.logical_and(z == 0, j == 0))
+        def _():
+            act(forward(slot, UP, src))
+
+        @pl.when(jnp.logical_and(z == Z - 1, j == 0))
+        def _():
+            act(forward(slot, DOWN, src))
+
+        @pl.when(jnp.logical_and(z == 1, j == 2))
+        def _():
+            act(forward(slot, DOWN, src, 1))
+
+        @pl.when(jnp.logical_and(z == 2, j == 2))
+        def _():
+            act(forward(slot, UP, src, 1))
+
+        act(forward(slot, SIBLING, src))
 
     def begin(kind, slot, copy):
         if kind == "enter":
@@ -224,7 +264,7 @@
                 @pl.when(q >= 2)
                 def _():
                     landed(k, slot)
-                    forward(slot, SIBLING, x.at[k, rows(slot)]).start()
+                    cross(j, slot, lambda copy: copy.start())
 
             landed(sib, slot)
             process(slot)
@@ -400,7 +440,7 @@
     if Y == 2:
         def drain_side(zz, c):
             slot = zz * Y + (1 - y)
-            forward(slot, SIBLING, x.at[k, rows(slot)]).wait_send()
+            cross(jnp.abs(zz - z), slot, lambda copy: copy.wait_send())
             return c
 
         lax.fori_loop(0, Z, drain_side, 0)

time: 117 us -> 112 us (0.957)
  Pallas kernels: 105 us -> 99.6 us
    pallas_call x1, Pallas kernels: 105 us -> 99.6 us  [body(): pl.pallas_call(functools.partial(kernel, Z, Y, scale), out_shape=(jax.Sha...]
where the time goes in v2:
time: 112 us
  Pallas kernels  99.6 us (89%)
  local copies, waits for them, and re-layouts  9.56 us (9%)
  between operations  1.95 us (2%)
    pallas_call x1, Pallas kernels, body(): pl.pallas_call(functools.partial(kernel, Z, Y, scale), out_shape=(jax.Sha...  99.6 us
    unnamed x4, local copies, waits for them, and re-layouts  8.96 us

profile of v2, /device:TPU:0, one launch (start us, length us, event | category | flops | bytes accessed | tf_op | source)
XLA Modules:
  0.0 111.9 jit_solution(9802373443013979823)
XLA Ops:
  1.9 0.8 convert_bitcast_fusion
  2.7 0.6 concatenate.3.meta
  3.3 99.6 %shard_map.68 = (f32[2048,1024]{1,0:T(8,128)}, f32[1,128]{1,0:T(1,128)}) custom-call(bf16[128,2048]{1,0:T(8,128)(2,1)} %features.1, f32[2048,1024]{1,0:T(8,128)} %weights.1, f32[8,128]{1,0:T(8,128)} %concatenate.3.meta, s32[1]{0:T(128)} %copy.10.active), custom_call_target="tpu_custom_call" | custom-call | tf_op jit(solution)/shard_map/pallas_call | solution.py:491
  102.9 0.0 copy-start
  102.9 8.4 %copy.11 = f32[2048,1024]{1,0:T(8,128)} copy(f32[2048,1024]{1,0:T(8,128)} %get-tuple-element.8) | data formatting | bytes 16777216
  111.4 0.0 copy-done
  111.4 0.5 copy.12
Async XLA Ops:
  102.9 8.5 %copy-start = (f32[1,128]{1,0:T(1,128)S(1)}, f32[1,128]{1,0:T(1,128)}, u32[]{:S(2)}) copy-start(f32[1,128]{1,0:T(1,128)} %get-tuple-element.5) | copy-start | bytes 1540

commit v3 on v2

--- a/solution.py
+++ b/solution.py
@@ -58,16 +58,24 @@
 
     barrier = pltpu.get_barrier_semaphore()
 
-    def greet(p, c):
-        peer = lax.rem(mine + p, nd)
+    def greet(example, core):
         pl.semaphore_signal(
-            barrier, inc=1, device_id={"example": peer // 2, "cls": lax.rem(peer, 2)},
-            device_id_type=MESH,
-        )
-        return c
-
-    lax.fori_loop(1, nd, greet, 0)
-    pl.semaphore_wait(barrier, nd - 1)
+            barrier, inc=1, device_id={"example": example, "cls": core}, device_id_type=MESH
+        )
+
+    greet(me, sib)
+    if Y == 2:
+        greet(z * Y + (1 - y), k)
+
+    @pl.when(z < Z - 1)
+    def _():
+        greet(me + Y, k)
+
+    @pl.when(z > 0)
+    def _():
+        greet(me - Y, k)
+
+    pl.semaphore_wait(barrier, Y + (z < Z - 1).astype(jnp.int32) + (z > 0).astype(jnp.int32))
 
     def forward(slot, direction, src, second=None):
         place = rows(slot)
@@ -174,7 +182,6 @@
             copy.wait_send()
 
     line(0, begin_own, own=True)
-    lax.fori_loop(1, n, meta_start, 0)
     w_send = remote(weights.at[:, columns(sib)], w.at[k], wsend, wrecv, me, sib)
     w_send.start()
 
@@ -199,7 +206,6 @@
         remote(meta, meta_all.at[src], msend.at[p], mrecv.at[src], me, sib).wait_recv()
         return c
 
-    lax.fori_loop(1, n, meta_wait, 0)
 
     active_count = active[0]
     class_base = mine * ck
@@ -304,6 +310,10 @@
             lambda: lax.fori_loop(1, nd, wait_out, 0),
         )
 
+    start1, in1, out1 = share(stat1, None, ssend.at[0], srecv.at[0])
+    start1()
+    lax.fori_loop(1, n, meta_start, 0)
+    lax.fori_loop(1, n, meta_wait, 0)
     counts = meta_all[:, 1, :]
     valid_total = jnp.sum(counts[:, 0:1], axis=0, keepdims=True)
 
@@ -333,10 +343,8 @@
                 acc = acc + jnp.sum(row_sum * ssq[rows(i), 0:1], axis=0, keepdims=True)
             return acc
 
-        return lax.fori_loop(0, n, go, jnp.zeros((1, 1), F32))
-
-    start1, in1, out1 = share(stat1, None, ssend.at[0], srecv.at[0])
-    start1()
+        return lax.fori_loop(0, n, go, jnp.zeros((1, 1), F32), unroll=4)
+
     in1()
     combine(stat1)
     fisher_part = residuals(True)
@@ -355,7 +363,7 @@
         g_scr[h, part, :] = jnp.dot(xt[h, part, :], r_scr[...], preferred_element_type=F32)
         return c
 
-    lax.fori_loop(0, 2 * per_half, gradient, 0)
+    lax.fori_loop(0, 2 * per_half, gradient, 0, unroll=2)
 
     in_d()
     fisher_sum = damp_all[0, 0:1, 0:1]
@@ -364,8 +372,12 @@
     damping = DAMPING_SHARE * fisher_sum / scale + EPSILON
     e_scr[...] = jnp.zeros_like(e_scr)
 
+    big = min(1024, half)
+    parts = half // big
+
     def fisher_step(i, c):
-        h, part = chunk(i)
+        h = i // parts
+        part = pl.ds(pl.multiple_of(lax.rem(i, parts) * big, big), big)
         block = xt[h, part, :]
         fisher = jnp.dot(block * block, fw_scr[...], preferred_element_type=F32)
         inverse = 1.0 / (fisher + damping)
@@ -377,13 +389,13 @@
         e_scr[...] += jnp.dot(x[h, :, part], low, preferred_element_type=F32)
         return c
 
-    lax.fori_loop(0, 2 * per_half, fisher_step, 0)
+    lax.fori_loop(0, 2 * parts, fisher_step, 0)
 
     def second(i, c):
         statistics(i, e_scr[rows(i), :], stat2, True)
         return c
 
-    lax.fori_loop(0, n, second, 0)
+    lax.fori_loop(0, n, second, 0, unroll=4)
     start2, in2, out2 = share(stat2, None, ssend.at[1], srecv.at[1])
     start2()
     in2()

time: 112 us -> 105 us (0.938)
  Pallas kernels: 99.6 us -> 92 us
    pallas_call x1, Pallas kernels: 99.6 us -> 92 us  [body(): pl.pallas_call(functools.partial(kernel, Z, Y, scale), out_shape=(jax.Sha...]
where the time goes in v3:
time: 105 us; the launch traced here: 104 us
  Pallas kernels  92 us (88%)
  local copies, waits for them, and re-layouts  9.56 us (9%)
  between operations  1.95 us (2%)
    pallas_call x1, Pallas kernels, body(): pl.pallas_call(functools.partial(kernel, Z, Y, scale), out_shape=(jax.Sha...  92 us
    unnamed x4, local copies, waits for them, and re-layouts  8.96 us

profile of v3, /device:TPU:0, one launch (start us, length us, event | category | flops | bytes accessed | tf_op | source)
XLA Modules:
  0.0 104.2 jit_solution(13744569552175909793)
XLA Ops:
  1.9 0.8 convert_bitcast_fusion
  2.7 0.6 concatenate.3.meta
  3.3 92.0 %shard_map.68 = (f32[2048,1024]{1,0:T(8,128)}, f32[1,128]{1,0:T(1,128)}) custom-call(bf16[128,2048]{1,0:T(8,128)(2,1)} %features.1, f32[2048,1024]{1,0:T(8,128)} %weights.1, f32[8,128]{1,0:T(8,128)} %concatenate.3.meta, s32[1]{0:T(128)} %copy.10.active), custom_call_target="tpu_custom_call" | custom-call | tf_op jit(solution)/shard_map/pallas_call | solution.py:503
  95.3 0.0 copy-start
  95.3 8.4 %copy.11 = f32[2048,1024]{1,0:T(8,128)} copy(f32[2048,1024]{1,0:T(8,128)} %get-tuple-element.8) | data formatting | bytes 16777216
  103.7 0.0 copy-done
  103.7 0.5 copy.12
Async XLA Ops:
  95.3 8.5 %copy-start = (f32[1,128]{1,0:T(1,128)S(1)}, f32[1,128]{1,0:T(1,128)}, u32[]{:S(2)}) copy-start(f32[1,128]{1,0:T(1,128)} %get-tuple-element.5) | copy-start | bytes 1540
